TPU v7x, 32 devices: a whole 2x2x4 slice. The times are simulated.
32 devices in a mesh: gx: 16 (over z, y, core), ta: 2 (over x).
Axes of the slice: x: 2, y: 2, z: 4, core: 2. Of those that a mesh axis runs over, the one named last changes fastest.
Arguments:
- source: float32 [32, 512, 512], P('ta', 'gx'), may hold values from -6 to 6
- previous: float32 [32, 512, 512], P('ta', 'gx'), may hold values from -6 to 6
- time_modes: float32 [32, 32], replicated, as said below
- time_back: float32 [32, 32], replicated, as said below
- step_code: int32 [32], P('ta'), may hold values from 0 to 32
Outputs:
- next_iterate: float32 [32, 512, 512], P('ta', 'gx')
Inputs may be any that keep to these rules, and one draw needn't show every extreme that they name: time_modes times time_back is the identity up to rounding. time_back is the inverse of time_modes up to rounding.
All inputs are finite; a program needn't handle non-finite values.
Results may differ from a plain program's by a relative error of at most 0.0001.
Values sent between devices are 32-bit elements; how exact they have to be, the bound alone decides.
A program may use at most 64 MiB of HBM per device.

v0:
```python
import jax
import jax.numpy as jnp
from jax import lax
from jax.sharding import PartitionSpec as P

CY = 64
CZ = 8
CYCLES = 2
LEVELS = 3


ROBIN = 1.0
DAMPING = 0.8


def extended(block, sides, width):
    for axis, dim in sides:
        count = lax.axis_size(axis)
        forward = [(i, i + 1) for i in range(count - 1)]
        backward = [(target, source) for source, target in forward]
        low = lax.ppermute(
            lax.slice_in_dim(block, block.shape[dim] - width, None, axis=dim), axis, forward
        )
        high = lax.ppermute(lax.slice_in_dim(block, 0, width, axis=dim), axis, backward)
        block = jnp.concatenate([low, block, high], axis=dim)
    return block


def neighbour_sum(field, zdim, ydim):
    rank = field.ndim
    xpad = jnp.pad(field, [(0, 0)] * (rank - 2) + [(1, 1), (0, 0)])
    total = xpad[..., 2:, :] + xpad[..., :-2, :]
    zpad = jnp.pad(field, [(0, 0)] * (rank - 1) + [(ydim, ydim)])
    total = total + zpad[..., 2 * ydim :] + zpad[..., : -2 * ydim]
    ypad = jnp.pad(field, [(0, 0)] * (rank - 1) + [(1, 1)])
    column = jnp.arange(zdim * ydim) % ydim
    upper = (column != ydim - 1).astype(jnp.float32)
    lower = (column != 0).astype(jnp.float32)
    return total + upper * ypad[..., 2:] + lower * ypad[..., :-2]


def edge_weights(xdim, left, right):
    position = jnp.arange(xdim)[:, None]
    return left * (position == 0).astype(jnp.float32) + right * (position == xdim - 1).astype(
        jnp.float32
    )


def smooth(field, target, diag, scale, zdim, ydim, sweeps):
    for sweep in range(sweeps):
        applied = diag * field - scale * neighbour_sum(field, zdim, ydim)
        field = field + DAMPING * (target - applied) / diag
    return field


def plane_table(zdim, ydim):
    cells = jnp.arange(zdim * ydim)
    coarse_index = cells // ydim // 2 * (ydim // 2) + cells % ydim // 2
    targets = jnp.arange(zdim // 2 * (ydim // 2))
    return (coarse_index[:, None] == targets[None, :]).astype(jnp.float32)


def restrict(field, zdim, ydim):
    modes, groups, xdim, plane = field.shape
    paired = jnp.sum(field.reshape(modes, groups, xdim // 2, 2, plane), axis=3)
    table = plane_table(zdim, ydim) * 0.125
    return jnp.einsum("mgxc,cd->mgxd", paired, table, precision=lax.Precision.HIGHEST)


def prolong(field, zdim, ydim):
    modes, groups, xdim, plane = field.shape
    table = plane_table(zdim, ydim)
    spread = jnp.einsum("mgxd,cd->mgxc", field, table, precision=lax.Precision.HIGHEST)
    spread = jnp.broadcast_to(spread[:, :, :, None, :], (modes, groups, xdim, 2, zdim * ydim))
    return spread.reshape(modes, groups, 2 * xdim, zdim * ydim)


def vcycle(field, target, shifts, left, right, level, zdim, ydim):
    scale = 0.25**level
    edge = edge_weights(field.shape[2], left, right)
    diag = shifts + scale * (6.0 + edge)
    if level == LEVELS - 1:
        return smooth(field, target, diag, scale, zdim, ydim, 6)
    field = smooth(field, target, diag, scale, zdim, ydim, 2)
    resid = target - (diag * field - scale * neighbour_sum(field, zdim, ydim))
    coarse_target = restrict(resid, zdim, ydim)
    coarse = vcycle(
        jnp.zeros_like(coarse_target),
        coarse_target,
        shifts,
        left,
        right,
        level + 1,
        zdim // 2,
        ydim // 2,
    )
    field = field + prolong(coarse, zdim, ydim)
    return smooth(field, target, diag, scale, zdim, ydim, 2)


def solve_modes(target, shifts, left, right):
    field = jnp.zeros_like(target)
    for cycle in range(CYCLES):
        field = vcycle(field, target, shifts, left, right, 0, CZ, CY)
    return field


def body(source, previous, time_modes, time_back, step_code):
    block_steps = source.shape[0]
    group_index = lax.axis_index("gx")
    group_count = lax.axis_size("gx")
    has_left = (group_index > 0).astype(jnp.float32)
    has_right = (group_index < group_count - 1).astype(jnp.float32)
    padded = extended(previous, (("gx", 1),), 1)
    trace_left = has_left * (padded[:, 0, :] - ROBIN * previous[:, 0, :])
    trace_right = has_right * (padded[:, -1, :] - ROBIN * previous[:, -1, :])
    rhs = source.at[:, 0, :].add(trace_left).at[:, -1, :].add(trace_right)
    own_start = lax.axis_index("ta") * block_steps
    own_columns = lax.dynamic_slice_in_dim(time_modes, own_start, block_steps, 1)
    modes = lax.psum_scatter(
        jnp.einsum("mt,txc->mxc", own_columns, rhs, precision=lax.Precision.HIGHEST),
        "ta",
        scatter_dimension=0,
        tiled=True,
    )
    shifts = (0.05 * jnp.exp2(step_code.astype(jnp.float32) / 4.0)).reshape(block_steps, 1, 1, 1)
    left = (ROBIN * has_left).reshape(1, 1, 1, 1)
    right = (ROBIN * has_right).reshape(1, 1, 1, 1)
    solved = solve_modes(modes[:, None], shifts, left, right)[:, 0]
    own_rows = lax.dynamic_slice_in_dim(time_back, own_start, block_steps, 0)
    return jnp.einsum(
        "tm,mxc->txc",
        own_rows,
        lax.all_gather(solved, "ta", axis=0, tiled=True),
        precision=lax.Precision.HIGHEST,
    )


def solution(mesh):
    placed = (P("ta", "gx", None), P("ta", "gx", None), P(), P(), P("ta"))
    return jax.shard_map(
        body, mesh=mesh, in_specs=placed, out_specs=P("ta", "gx", None), check_vma=False
    )
```

profile of v0, /device:TPU:0, one launch (start us, length us, event | category | flops | bytes accessed | tf_op | source)
XLA Modules:
  0.0 131.2 jit_solution(1484397922064622471)
XLA Ops:
  6.5 1.2 copy.46
  7.8 1.0 slice.605
  8.8 2.4 %collective-permute-start = (f32[16,1,512]{2,1,0:T(1,128)S(1)}, f32[16,1,512]{2,1,0:T(1,128)S(1)}, u32[]{:S(2)}, u32[]{:S(2)}) collective-permute-start(f32[16,1,512]{2,1,0:T(1,128)S(1)} %slice.605), channel_id=1, source_target_pairs={{0,2},{2,4},{4,6},{6,8},{8,10},{10,12},{12,14},{14,16},{16,18},{18... | collective-permute-start | bytes 98312 | tf_op jit(solution)/shard_map/ppermute | solution.py:21
  11.2 0.8 collective-permute-done
  12.0 1.0 fusion.445
  13.0 1.3 collective-permute-start.1
  14.3 0.1 scatter-add.6
  14.5 3.9 %collective-permute-done.1 = f32[16,1,512]{2,1,0:T(1,128)S(1)} collective-permute-done((f32[16,1,512]{2,1,0:T(1,128)S(1)}, f32[16,1,512]{2,1,0:T(1,128)S(1)}, u32[]{:S(2)}, u32[]{:S(2)}) %collective-permute-start.1) | collective-permute-done | bytes 32800 | tf_op jit(solution)/shard_map/ppermute | solution.py:24
  18.4 1.0 slice_add_fusion
  19.4 0.1 scatter-add.9
  19.6 3.5 %fusion.115 = f32[32,32,512]{2,0,1:T(8,128)} fusion(f32[16,32,512]{2,1,0:T(8,128)S(1)} %scatter-add.9, f32[32,32]{1,0:T(8,128)S(1)} %copy-done, s32[]{:T(128)S(6)} %select_n.356), kind=kOutput, calls=%fused_computation.179 | convolution fusion | flops 100663296 | bytes 3149828 | tf_op jit(solution)/shard_map/mt,txc->mxc/dot_general | solution.py:121
  23.2 0.2 all-gather.3.cloned.1.call-start
  23.5 0.3 copy-done.3
  23.8 0.1 broadcast_multiply_fusion.2
  24.0 35.2 %reduce-scatter.2.cloned.1.call-done = f32[16,32,512]{2,0,1:T(8,128)} async-done(((f32[32,32,512]{2,0,1:T(8,128)}), f32[16,32,512]{2,0,1:T(8,128)}) %reduce-scatter.2.cloned.1.call-update) | async-done | bytes 1048592 | tf_op jit(solution)/shard_map/reduce_scatter | solution.py:120
  59.2 0.1 broadcast_in_dim.24
  59.4 1.1 copy-done.1
  60.5 1.3 %fusion.112 = f32[16,1,32,512]{3,0,2,1:T(8,128)S(1)} fusion(f32[16,1,32,512]{3,0,2,1:T(8,128)S(1)} %broadcast_in_dim.24, f32[16,32,512]{2,0,1:T(8,128)S(1)} %copy-done.1, f32[16,32]{0,1:T(8,128)S(1)} %get-tuple-element.36, f32[512]{0:T(512)S(1)} %get-tuple-element.46, f32[512]{0:T(512)S(1)} %get-tuple-element.45, f32[16,32]{0,1:T(8,128)S(1)} %get-tuple-element.35), kind=kLoop, calls=%fused_computation.174 | loop fusion | flops 2883584 | bytes 3153920 | tf_op jit(solution)/shard_map/div | solution.py:52
  61.8 1.3 fusion.11
  63.1 1.2 fusion.18
  64.3 0.9 reduce_sum.36
  65.2 1.7 %fusion.119 = f32[16,16,128]{2,0,1:T(8,128)S(1)} fusion(f32[16,16,512]{2,0,1:T(8,128)} %reduce_sum.36, s32[512]{0:T(512)S(1)} %fusion.411), kind=kOutput, calls=%fused_computation.221 | convolution fusion | flops 201457664 | bytes 657408 | tf_op jit(solution)/shard_map/mgxc,cd->mgxd/dot_general | solution.py:67
  66.9 0.3 fusion.238
  67.2 0.2 fusion.138
  67.5 0.2 fusion.146
  67.7 0.2 reduce_sum.37
  67.9 0.2 multiply_divide_fusion.1
  68.1 0.2 fusion.269
  68.3 0.2 fusion.280
  68.4 0.2 fusion.291
  68.6 0.2 fusion.302
  68.8 0.3 fusion.372
  69.2 0.2 fusion.157
  69.4 0.2 fusion.250
  69.7 0.5 fusion.126
  70.2 0.1 broadcast_in_dim.27
  70.3 0.2 bitcast_add_fusion.1
  70.5 1.3 fusion.28
  71.8 1.3 fusion.38
  73.1 1.3 fusion.48
  74.4 1.5 %fusion.58 = f32[16,1,32,512]{3,0,2,1:T(8,128)S(1)} fusion(f32[16,1,32,512]{3,0,2,1:T(8,128)S(1)} %fusion.48, f32[16,32,512]{2,0,1:T(8,128)S(1)} %copy-done.1, f32[16,32]{0,1:T(8,128)S(1)} %get-tuple-element.36, f32[512]{0:T(512)S(1)} %get-tuple-element.46, f32[512]{0:T(512)S(1)} %get-tuple-element.45), kind=kLoop, calls=%fused_computation.120 | loop fusion | flops 3407872 | bytes 3151872 | tf_op jit(solution)/shard_map/add | solution.py:52
  75.9 1.2 fusion.65
  77.1 0.9 reduce_sum.38
  78.0 1.7 %fusion.117 = f32[16,16,128]{2,0,1:T(8,128)S(1)} fusion(f32[16,16,512]{2,0,1:T(8,128)} %reduce_sum.38, s32[512]{0:T(512)S(1)} %fusion.411), kind=kOutput, calls=%fused_computation.219 | convolution fusion | flops 201457664 | bytes 657408 | tf_op jit(solution)/shard_map/mgxc,cd->mgxd/dot_general | solution.py:67
  79.7 0.3 fusion.236
  80.0 0.2 fusion.179
  80.2 0.2 fusion.187
  80.5 0.2 reduce_sum.39
  80.6 0.2 multiply_divide_fusion
  80.9 0.2 fusion.324
  81.0 0.2 fusion.335
  81.2 0.2 fusion.346
  81.4 0.2 fusion.357
  81.5 0.3 fusion.370
  81.9 0.2 fusion.198
  82.2 0.2 fusion.249
  82.4 0.5 fusion.124
  82.9 0.1 broadcast_in_dim.31
  83.0 0.2 bitcast_add_fusion
  83.3 1.3 fusion.75
  84.6 2.2 %fusion.85 = f32[16,1,32,512]{3,0,2,1:T(8,128)} fusion(f32[16,1,32,512]{3,0,2,1:T(8,128)S(1)} %fusion.75, f32[16,32,512]{2,0,1:T(8,128)S(1)} %copy-done.1, f32[16,32]{0,1:T(8,128)S(1)} %get-tuple-element.36, f32[512]{0:T(512)S(1)} %get-tuple-element.46, f32[512]{0:T(512)S(1)} %get-tuple-element.45), kind=kLoop, calls=%fused_computation.147 | loop fusion | flops 3407872 | bytes 3151872 | tf_op jit(solution)/shard_map/add | solution.py:52
  86.8 33.3 %all-gather.3.cloned.1.call-done = f32[32,1,32,512]{3,0,2,1:T(8,128)} async-done(((f32[16,1,32,512]{3,0,2,1:T(8,128)}), f32[32,1,32,512]{3,0,2,1:T(8,128)}) %all-gather.3.cloned.1.call-update) | async-done | bytes 2097168 | tf_op jit(solution)/shard_map/all_gather | solution.py:134
  120.1 2.7 %fusion = f32[16,32,512]{2,0,1:T(8,128)S(1)} fusion(f32[32,1,32,512]{3,0,2,1:T(8,128)} %all-gather.3.cloned.1.call-done, f32[32,32]{1,0:T(8,128)S(1)} %copy-done.2, s32[]{:T(128)S(6)} %select_n.356), kind=kOutput, calls=%fused_computation | convolution fusion | flops 100663296 | bytes 3153924 | tf_op jit(solution)/shard_map/tm,mxc->txc/dot_general | solution.py:131
  122.8 1.6 %copy.17 = f32[16,32,512]{2,1,0:T(8,128)} copy(f32[16,32,512]{2,0,1:T(8,128)S(1)} %fusion) | data formatting | bytes 2097152 | tf_op jit(solution)/shard_map/tm,mxc->txc/dot_general | solution.py:131
  (26 shorter events, 0.4 us)
Async XLA Ops:
  6.5 13.0 %copy-start = (f32[32,32]{1,0:T(8,128)S(1)}, f32[32,32]{1,0:T(8,128)}, u32[]{:S(2)}) copy-start(f32[32,32]{1,0:T(8,128)} %param.11) | copy-start | bytes 12292
  6.5 52.7 %reduce-scatter.2.cloned.1.call-start = ((), (), s32[]{:S(2)}) async-start(), calls=%async_computation.1 | async-start | bytes 3145728 | tf_op jit(solution)/shard_map/reduce_scatter | solution.py:120
  8.8 3.2 %collective-permute-start = (f32[16,1,512]{2,1,0:T(1,128)S(1)}, f32[16,1,512]{2,1,0:T(1,128)S(1)}, u32[]{:S(2)}, u32[]{:S(2)}) collective-permute-start(f32[16,1,512]{2,1,0:T(1,128)S(1)} %slice.605), channel_id=1, source_target_pairs={{0,2},{2,4},{4,6},{6,8},{8,10},{10,12},{12,14},{14,16},{16,18},{18... | collective-permute-start | bytes 98312 | tf_op jit(solution)/shard_map/ppermute | solution.py:21
  13.0 5.4 %collective-permute-start.1 = (f32[16,1,512]{2,1,0:T(1,128)S(1)}, f32[16,1,512]{2,1,0:T(1,128)S(1)}, u32[]{:S(2)}, u32[]{:S(2)}) collective-permute-start(f32[16,1,512]{2,1,0:T(1,128)S(1)} %get-tuple-element.29), channel_id=1, source_target_pairs={{2,0},{4,2},{6,4},{8,6},{10,8},{12,10},{14,12},{16,14},{18,16},{20... | collective-permute-start | bytes 98312 | tf_op jit(solution)/shard_map/ppermute | solution.py:24
  23.1 0.7 copy-start.3
  23.2 96.9 %all-gather.3.cloned.1.call-start = ((), (), s32[]{:S(2)}) async-start(), calls=%async_computation.2 | async-start | bytes 3145728 | tf_op jit(solution)/shard_map/all_gather | solution.py:134
  59.2 1.2 copy-start.1
  84.5 35.5 %copy-start.2 = (f32[32,32]{1,0:T(8,128)S(1)}, f32[32,32]{1,0:T(8,128)}, u32[]{:S(2)}) copy-start(f32[32,32]{1,0:T(8,128)} %param.12) | copy-start | bytes 12292
Sparse Core Ops, SparseCore 0:
  23.3 35.9 reduce-scatter.1
  86.9 33.0 all-gather.2
where the time goes:
time: 132 us; the launch traced here: 131 us
  waiting for transfers between devices  73.3 us (56%)
  other arithmetic  22.6 us (17%)
  between operations  13.9 us (11%)
  matrix products  11.6 us (9%)
  local copies, waits for them, and re-layouts  5.96 us (5%)
  starting transfers between devices  3.92 us (3%)
    reduce_scatter x1, waiting for transfers between devices, body(): lax.psum_scatter(jnp.einsum('mt,txc->mxc', own_columns, rhs, precision=la...  35.2 us
    all_gather x1, waiting for transfers between devices, body(): lax.all_gather(solved, 'ta', axis=0, tiled=True)  33.3 us
    add x19, other arithmetic, smooth(): field = field + DAMPING * (target - applied) / diag  12.4 us
    ppermute x1, waiting for transfers between devices, extended(): lax.ppermute(lax.slice_in_dim(block, 0, width, axis=dim), axis, backward)  3.92 us
    dot_general x4, matrix products, restrict(): jnp.einsum('mgxc,cd->mgxd', paired, table, precision=lax.Precision.HIGHEST)  3.77 us
    dot_general x1, matrix products, body(): jnp.einsum('mt,txc->mxc', own_columns, rhs, precision=lax.Precision.HIGHEST)  3.55 us
    sub x4, other arithmetic, vcycle(): resid = target - (diag * field - scale * neighbour_sum(field, zdim, ydim))  2.91 us
    dot_general x1, matrix products, body(): jnp.einsum('tm,mxc->txc', own_rows, lax.all_gather(solved, 'ta', axis=0,...  2.7 us
  transfers between devices with their start and end apart: 4, of which 4 were waited for; matrix products, arithmetic and copies ran while one was open for 0% of the time, Pallas kernels for 0%

commit v1 on v0

v1 whole, which is shorter than its diff:
```python
import functools

import jax
import jax.numpy as jnp
from jax import lax
from jax.experimental import pallas as pl
from jax.experimental.pallas import tpu as pltpu
from jax.sharding import PartitionSpec as P

CY = 64
CZ = 8
CYCLES = 2

ROBIN = 1.0
DAMPING = 0.8

SUB = 8
LANES = 128
PAIRS = SUB // 2
GROUP = LANES // PAIRS
MESH = pl.DeviceIdType.MESH
HIGHEST = lax.Precision.HIGHEST


def spread(matrix, steps):
    wide = jnp.concatenate([matrix] * SUB, axis=1)
    rows = steps * SUB
    tall = jnp.broadcast_to(wide[:, None, :], (steps, SUB, SUB * GROUP)).reshape(rows, SUB * GROUP)
    row = lax.broadcasted_iota(jnp.int32, (rows, SUB * GROUP), 0) % SUB
    lane = lax.broadcasted_iota(jnp.int32, (rows, SUB * GROUP), 1)
    want = (lane % LANES) // GROUP * 2 + lane // LANES
    return jnp.where(row == want, tall, 0.0)


def each(count, action):
    if count == 1:
        action(0)
    else:
        lax.fori_loop(0, count, lambda i, carry: (action(i), carry)[1], 0)


def gather_kernel(
    peers, groups_gx, src, prev, shift, table, f_out, shift_out,
    held, near_left, near_right, first, last, weights,
    send_in, recv_in, send_lo, recv_lo, send_hi, recv_hi, send_sh, recv_sh,
    halo_send, halo_recv, local,
):
    steps, cells_x, plane = src.shape
    chunks = cells_x // SUB
    me = lax.axis_index("ta")
    spot = lax.axis_index("gx")
    has_left = spot > 0
    has_right = spot < groups_gx - 1

    barrier = pltpu.get_barrier_semaphore()
    for d in range(1, peers):
        pl.semaphore_signal(
            barrier, inc=1, device_id={"ta": lax.rem(me + d, peers)}, device_id_type=MESH
        )

    @pl.when(has_left)
    def _():
        pl.semaphore_signal(barrier, inc=1, device_id={"gx": spot - 1}, device_id_type=MESH)

    @pl.when(has_right)
    def _():
        pl.semaphore_signal(barrier, inc=1, device_id={"gx": spot + 1}, device_id_type=MESH)

    own = [
        pltpu.make_async_copy(src, held.at[me], local.at[0]),
        pltpu.make_async_copy(prev.at[:, 0:SUB, :], first, local.at[1]),
        pltpu.make_async_copy(prev.at[:, cells_x - SUB : cells_x, :], last, local.at[2]),
    ]
    for copy in own:
        copy.start()

    sides = has_left.astype(jnp.int32) + has_right.astype(jnp.int32)
    pl.semaphore_wait(barrier, peers - 1 + sides)

    def remote(source, target, send, recv, where):
        return pltpu.make_async_remote_copy(
            src_ref=source, dst_ref=target, send_sem=send, recv_sem=recv,
            device_id=where, device_id_type=MESH,
        )

    to_left = remote(
        prev.at[:, 0:SUB, :], near_right, halo_send.at[0], halo_recv.at[0], {"gx": spot - 1}
    )
    to_right = remote(
        prev.at[:, cells_x - SUB : cells_x, :], near_left, halo_send.at[1], halo_recv.at[1],
        {"gx": spot + 1},
    )

    @pl.when(has_left)
    def _():
        to_left.start()

    @pl.when(has_right)
    def _():
        to_right.start()

    inner = []
    for d in range(1, peers):
        where = {"ta": lax.rem(me + d, peers)}
        inner.append(remote(shift, shift_out.at[me], send_sh.at[d], recv_sh.at[d], where))
        inner.append(
            remote(
                src.at[:, SUB : cells_x - SUB, :],
                held.at[me, :, SUB : cells_x - SUB, :],
                send_in.at[d], recv_in.at[d], where,
            )
        )
    for copy in inner:
        copy.start()
    shift_out[me] = shift[...]

    def weigh(part):
        for block in range(peers):
            rows = table[part, :, block * steps : (block + 1) * steps]
            weights[part, block] = spread(rows.T, steps)

    each(f_out.shape[0], weigh)

    for copy in own:
        copy.wait()

    row = lax.broadcasted_iota(jnp.int32, (steps, SUB, plane), 1)

    @pl.when(has_right)
    def _():
        to_right.wait_send()
        pltpu.make_async_copy(near_right, near_right, halo_recv.at[0]).wait()
        trace = near_right[:, 0:1, :] - ROBIN * last[:, SUB - 1 : SUB, :]
        block = held[me, :, cells_x - SUB : cells_x, :]
        held[me, :, cells_x - SUB : cells_x, :] = block + jnp.where(row == SUB - 1, trace, 0.0)

    @pl.when(has_left)
    def _():
        to_left.wait_send()
        pltpu.make_async_copy(near_left, near_left, halo_recv.at[1]).wait()
        trace = near_left[:, SUB - 1 : SUB, :] - ROBIN * first[:, 0:1, :]
        block = held[me, :, 0:SUB, :]
        held[me, :, 0:SUB, :] = block + jnp.where(row == 0, trace, 0.0)

    def transform(who, chunk, start):
        block = held[who, :, chunk * SUB : (chunk + 1) * SUB, :].reshape(steps * SUB, plane)

        def one(part):
            term = lax.dot_general(
                block, weights[part, who], (((0,), (0,)), ((), ())), precision=HIGHEST,
                preferred_element_type=jnp.float32,
            )
            for half in range(2):
                piece = term[:, half * LANES : (half + 1) * LANES].reshape(f_out.shape[3:])
                if start:
                    f_out[part, chunk, half] = piece
                else:
                    f_out[part, chunk, half] += piece

        each(f_out.shape[0], one)

    for chunk in range(1, chunks - 1):
        transform(me, chunk, True)

    outer = []
    for d in range(1, peers):
        where = {"ta": lax.rem(me + d, peers)}
        outer.append((
            remote(held.at[me, :, 0:SUB, :], held.at[me, :, 0:SUB, :],
                   send_lo.at[d], recv_lo.at[d], where),
            remote(held.at[me, :, cells_x - SUB : cells_x, :],
                   held.at[me, :, cells_x - SUB : cells_x, :],
                   send_hi.at[d], recv_hi.at[d], where),
        ))
    for low, high in outer:
        low.start()
        high.start()

    transform(me, 0, True)
    transform(me, chunks - 1, True)

    for copy in inner:
        copy.wait()
    for d in range(1, peers):
        who = lax.rem(me - d + peers, peers)
        for chunk in range(1, chunks - 1):
            transform(who, chunk, False)
    for d, (low, high) in enumerate(outer, 1):
        who = lax.rem(me - d + peers, peers)
        low.wait()
        transform(who, 0, False)
        high.wait()
        transform(who, chunks - 1, False)


def solve_kernel(peers, groups_gx, f_ref, shift, table, out, va, vb, g1, u1a, u1b, g2, u2a, u2b, fold, fold1, up1, up0):
    parts, chunks, _, zdim, ydim, _ = f_ref.shape
    steps = out.shape[0]
    me = lax.axis_index("ta")
    spot = lax.axis_index("gx")
    left = jnp.where(spot > 0, ROBIN, 0.0).astype(jnp.float32)
    right = jnp.where(spot < groups_gx - 1, ROBIN, 0.0).astype(jnp.float32)
    lane = lax.broadcasted_iota(jnp.int32, (SUB, LANES), 1)
    lane_mode = lane % GROUP
    zero = jnp.zeros((SUB, LANES), jnp.float32)
    z1, y1, z2, y2 = zdim // 2, ydim // 2, zdim // 4, ydim // 4

    def clear(ref, lead, zn, yn):
        def body(z, carry):
            for index in lead:
                ref[index + (z,)] = jnp.zeros((yn + 2 * SUB, LANES), jnp.float32)
            return carry
        for z in (0, zn + 1):
            body(z, 0)

        def edges(z, carry):
            for index in lead:
                ref[index + (z, slice(0, SUB))] = zero
                ref[index + (z, slice(SUB + yn, yn + 2 * SUB))] = zero
            return carry
        lax.fori_loop(1, zn + 1, edges, 0)

    lead0 = [(g, b) for g in range(chunks) for b in range(2)]
    lead1 = [(g,) for g in range(chunks)]
    for ref in (va, vb):
        clear(ref, lead0, zdim, ydim)
    for ref in (u1a, u1b):
        clear(ref, lead1, z1, y1)
    for ref in (u2a, u2b):
        clear(ref, lead1, z2, y2)

    def near(ref, index, z, y):
        base = SUB + y
        return (
            ref[index + (z + 1, slice(base - 1, base - 1 + SUB))]
            + ref[index + (z + 1, slice(base + 1, base + 1 + SUB))]
            + ref[index + (z, slice(base, base + SUB))]
            + ref[index + (z + 2, slice(base, base + SUB))]
        )

    def center(ref, index, z, y):
        return ref[index + (z + 1, slice(SUB + y, 2 * SUB + y))]

    def around0(ref, z, y):
        cur = {i: center(ref, i, z, y) for i in lead0}
        down = [pltpu.roll(cur[g, 1], GROUP, 1) for g in range(chunks)]
        upper = [pltpu.roll(cur[g, 0], LANES - GROUP, 1) for g in range(chunks)]
        total = {}
        for g in range(chunks):
            low = jnp.where(lane < GROUP, down[g - 1] if g else zero, down[g])
            total[g, 0] = near(ref, (g, 0), z, y) + (cur[g, 1] + low)
            high = jnp.where(
                lane >= LANES - GROUP, upper[g + 1] if g < chunks - 1 else zero, upper[g]
            )
            total[g, 1] = near(ref, (g, 1), z, y) + (cur[g, 0] + high)
        return cur, total

    def around1(ref, z, y):
        cur = {i: center(ref, i, z, y) for i in lead1}
        down = [pltpu.roll(cur[g,], GROUP, 1) for g in range(chunks)]
        upper = [pltpu.roll(cur[g,], LANES - GROUP, 1) for g in range(chunks)]
        total = {}
        for g in range(chunks):
            low = jnp.where(lane < GROUP, down[g - 1] if g else zero, down[g])
            high = jnp.where(
                lane >= LANES - GROUP, upper[g + 1] if g < chunks - 1 else zero, upper[g]
            )
            total[g,] = near(ref, (g,), z, y) + (low + high)
        return cur, total

    def around2(ref, z, y):
        cur = {i: center(ref, i, z, y) for i in lead1}
        swap = [pltpu.roll(cur[g,], LANES // 2, 1) for g in range(chunks)]
        total = {}
        for g in range(chunks):
            side = jnp.where(
                lane < LANES // 2, swap[g - 1] if g else zero, swap[g + 1] if g < chunks - 1 else zero
            )
            total[g,] = near(ref, (g,), z, y) + (swap[g] + side)
        return cur, total

    def solve(part):
        width = GROUP // steps
        shifts = shift[part * width]
        for block in range(1, width):
            shifts = jnp.where(lane_mode >= block * steps, shift[part * width + block], shifts)

        def diagonals(scale, size):
            low = jnp.where(lane < size, left, 0.0)
            high = jnp.where(lane >= LANES - size, right, 0.0)
            plain = shifts + scale * 6.0
            return plain, shifts + scale * (6.0 + low), shifts + scale * (6.0 + high)

        d0, d0l, d0r = diagonals(1.0, GROUP)
        d1, d1l, d1r = diagonals(0.25, GROUP)
        d2, d2l, d2r = diagonals(0.0625, LANES // 2)
        diag0 = {i: d0 for i in lead0}
        diag0[0, 0] = d0l
        diag0[chunks - 1, 1] = d0r
        diag1 = {i: d1 for i in lead1}
        diag1[0,] = d1l
        diag1[chunks - 1,] = d1r
        diag2 = {i: d2 for i in lead1}
        diag2[0,] = d2l
        diag2[chunks - 1,] = d2r

        def table_of(diag):
            seen = {}
            out = {}
            for key, value in diag.items():
                if id(value) not in seen:
                    seen[id(value)] = DAMPING / value
                out[key] = seen[id(value)]
            return out

        w0, w1, w2 = table_of(diag0), table_of(diag1), table_of(diag2)

        def target0(i, z, y):
            return f_ref[(part,) + i + (z, slice(y, y + SUB))]

        def start0(dst):
            def body(z, carry):
                for y in range(0, ydim, SUB):
                    for i in lead0:
                        dst[i + (z + 1, slice(SUB + y, 2 * SUB + y))] = w0[i] * target0(i, z, y)
                return carry
            lax.fori_loop(0, zdim, body, 0)

        def sweep0(src, dst):
            def body(z, carry):
                for y in range(0, ydim, SUB):
                    cur, total = around0(src, z, y)
                    for i in lead0:
                        dst[i + (z + 1, slice(SUB + y, 2 * SUB + y))] = (
                            (1.0 - DAMPING) * cur[i] + w0[i] * (target0(i, z, y) + total[i])
                        )
                return carry
            lax.fori_loop(0, zdim, body, 0)

        def restrict0(src):
            def body(zc, carry):
                for y in range(0, ydim, SUB):
                    sums = [None] * chunks
                    for dz in range(2):
                        z = 2 * zc + dz
                        cur, total = around0(src, z, y)
                        for i in lead0:
                            r = target0(i, z, y) - (diag0[i] * cur[i] - total[i])
                            sums[i[0]] = r if sums[i[0]] is None else sums[i[0]] + r
                    for g in range(chunks):
                        fold[g, zc, y : y + SUB] = sums[g]
                for g in range(chunks):
                    g1[g, zc] = 0.125 * (
                        fold[g, zc, pl.ds(0, y1, stride=2), :] + fold[g, zc, pl.ds(1, y1, stride=2), :]
                    )
                return carry
            lax.fori_loop(0, z1, body, 0)

        def add0(ref):
            def body(zc, carry):
                for g in range(chunks):
                    value = center_all(u1a, g, zc, y1)
                    up0[g, zc, pl.ds(0, y1, stride=2), :] = value
                    up0[g, zc, pl.ds(1, y1, stride=2), :] = value
                for g in range(chunks):
                    for y in range(0, ydim, SUB):
                        extra = up0[g, zc, y : y + SUB]
                        for b in range(2):
                            for dz in range(2):
                                at = (g, b, 2 * zc + dz + 1, slice(SUB + y, 2 * SUB + y))
                                ref[at] = ref[at] + extra
                return carry
            lax.fori_loop(0, z1, body, 0)

        def center_all(ref, g, z, yn):
            return ref[g, z + 1, SUB : SUB + yn]

        def start(dst, target, w, zn, yn):
            for z in range(zn):
                for y in range(0, yn, SUB):
                    for i in lead1:
                        dst[i + (z + 1, slice(SUB + y, 2 * SUB + y))] = (
                            w[i] * target[i + (z, slice(y, y + SUB))]
                        )

        def sweep(around, src, dst, target, w, scale, zn, yn):
            for z in range(zn):
                for y in range(0, yn, SUB):
                    cur, total = around(src, z, y)
                    for i in lead1:
                        dst[i + (z + 1, slice(SUB + y, 2 * SUB + y))] = (1.0 - DAMPING) * cur[i] + w[
                            i
                        ] * (target[i + (z, slice(y, y + SUB))] + scale * total[i])

        def restrict1(src):
            for zc in range(z2):
                for y in range(0, y1, SUB):
                    sums = [None] * chunks
                    for dz in range(2):
                        z = 2 * zc + dz
                        cur, total = around1(src, z, y)
                        for i in lead1:
                            r = g1[i + (z, slice(y, y + SUB))] - (
                                diag1[i] * cur[i] - 0.25 * total[i]
                            )
                            sums[i[0]] = r if sums[i[0]] is None else sums[i[0]] + r
                    for g in range(chunks):
                        even = (lane // GROUP) % 2 == 0
                        other = jnp.where(
                            even,
                            pltpu.roll(sums[g], LANES - GROUP, 1),
                            pltpu.roll(sums[g], GROUP, 1),
                        )
                        fold1[g, zc, y : y + SUB] = sums[g] + other
                for g in range(chunks):
                    g2[g, zc] = 0.125 * (
                        fold1[g, zc, pl.ds(0, y2, stride=2), :] + fold1[g, zc, pl.ds(1, y2, stride=2), :]
                    )

        def add1(ref):
            for zc in range(z2):
                for g in range(chunks):
                    value = center_all(u2b, g, zc, y2)
                    up1[g, zc, pl.ds(0, y2, stride=2), :] = value
                    up1[g, zc, pl.ds(1, y2, stride=2), :] = value
                for g in range(chunks):
                    for y in range(0, y1, SUB):
                        extra = up1[g, zc, y : y + SUB]
                        for dz in range(2):
                            at = (g, 2 * zc + dz + 1, slice(SUB + y, 2 * SUB + y))
                            ref[at] = ref[at] + extra

        for cycle in range(CYCLES):
            if cycle == 0:
                start0(va)
            else:
                sweep0(vb, va)
            sweep0(va, vb)
            restrict0(vb)
            start(u1a, g1, w1, z1, y1)
            sweep(around1, u1a, u1b, g1, w1, 0.25, z1, y1)
            restrict1(u1b)
            start(u2a, g2, w2, z2, y2)
            here, there = u2a, u2b
            for _ in range(5):
                sweep(around2, here, there, g2, w2, 0.0625, z2, y2)
                here, there = there, here
            add1(u1b)
            sweep(around1, u1b, u1a, g1, w1, 0.25, z1, y1)
            sweep(around1, u1a, u1b, g1, w1, 0.25, z1, y1)
            for g in range(chunks):
                for z in range(z1):
                    u1a[g, z + 1, SUB : SUB + y1] = u1b[g, z + 1, SUB : SUB + y1]
            add0(vb)
            sweep0(vb, va)
            sweep0(va, vb)

        rows = pl.ds(pl.multiple_of(me * steps, steps), steps)
        weights = spread(table[part, rows], steps)
        for g in range(chunks):
            field = jnp.concatenate(
                [
                    vb[g, b, 1 : zdim + 1, SUB : SUB + ydim].reshape(zdim * ydim, LANES)
                    for b in range(2)
                ],
                axis=1,
            )
            term = lax.dot_general(
                weights, field, (((1,), (1,)), ((), ())), precision=HIGHEST,
                preferred_element_type=jnp.float32,
            ).reshape(steps, SUB, zdim * ydim)
            if parts > 1:
                out[:, g * SUB : (g + 1) * SUB, :] += term
            else:
                out[:, g * SUB : (g + 1) * SUB, :] = term

    if parts > 1:
        out[...] = jnp.zeros_like(out)
    each(parts, solve)


def body(mesh, source, previous, time_modes, time_back, step_code):
    steps, cells_x, plane = source.shape
    total = time_modes.shape[0]
    peers, groups_gx = mesh.shape["ta"], mesh.shape["gx"]
    chunks, parts = cells_x // SUB, total // GROUP
    shifts = 0.05 * jnp.exp2(step_code.astype(jnp.float32) / 4.0)
    shifts = jnp.broadcast_to(jnp.tile(shifts, LANES // steps)[None], (SUB, LANES))
    vmem = pl.BlockSpec(memory_space=pltpu.VMEM)
    anywhere = pl.BlockSpec(memory_space=pl.ANY)
    dma = pltpu.SemaphoreType.DMA
    f32 = jnp.float32
    field = (parts, chunks, 2, CZ, CY, LANES)
    target, every = pl.pallas_call(
        functools.partial(gather_kernel, peers, groups_gx),
        out_shape=(
            jax.ShapeDtypeStruct(field, f32),
            jax.ShapeDtypeStruct((peers, SUB, LANES), f32),
        ),
        in_specs=[anywhere, anywhere, vmem, vmem],
        out_specs=(vmem, vmem),
        scratch_shapes=[
            pltpu.VMEM((peers, steps, cells_x, plane), f32),
            pltpu.VMEM((steps, SUB, plane), f32),
            pltpu.VMEM((steps, SUB, plane), f32),
            pltpu.VMEM((steps, SUB, plane), f32),
            pltpu.VMEM((steps, SUB, plane), f32),
            pltpu.VMEM((parts, peers, steps * SUB, SUB * GROUP), f32),
        ] + [dma((peers,))] * 8 + [dma((2,)), dma((2,)), dma((3,))],
        compiler_params=pltpu.CompilerParams(
            collective_id=0, has_side_effects=True, vmem_limit_bytes=48 << 20
        ),
        name="gather",
    )(source, previous, shifts, time_modes.reshape(parts, GROUP, total))
    wide0 = (chunks, 2, CZ + 2, CY + 2 * SUB, LANES)
    wide1 = (chunks, CZ // 2 + 2, CY // 2 + 2 * SUB, LANES)
    wide2 = (chunks, CZ // 4 + 2, CY // 4 + 2 * SUB, LANES)
    slim1 = (chunks, CZ // 2, CY // 2, LANES)
    slim2 = (chunks, CZ // 4, CY // 4, LANES)
    up0 = (chunks, CZ // 2, CY, LANES)
    up1 = (chunks, CZ // 4, CY // 2, LANES)
    shapes = [wide0, wide0, slim1, wide1, wide1, slim2, wide2, wide2, up0, up1, up1, up0]
    return pl.pallas_call(
        functools.partial(solve_kernel, peers, groups_gx),
        out_shape=jax.ShapeDtypeStruct(source.shape, f32),
        in_specs=[vmem] * 3,
        out_specs=vmem,
        scratch_shapes=[pltpu.VMEM(shape, f32) for shape in shapes],
        compiler_params=pltpu.CompilerParams(vmem_limit_bytes=48 << 20),
        name="solve",
    )(target, every, time_back.reshape(total, parts, GROUP).swapaxes(0, 1))


def solution(mesh):
    placed = (P("ta", "gx", None), P("ta", "gx", None), P(), P(), P("ta"))
    return jax.shard_map(
        functools.partial(body, mesh), mesh=mesh, in_specs=placed,
        out_specs=P("ta", "gx", None), check_vma=False,
    )
```

time: 132 us -> 51.7 us (0.39)
  waiting for transfers between devices: 73.3 us -> 0 us
  Pallas kernels: 0 us -> 47.2 us
  other arithmetic: 22.6 us -> 0.67 us
  between operations: 13.9 us -> 0.03 us
  matrix products: 11.6 us -> 0 us
  starting transfers between devices: 3.92 us -> 0 us
  local copies, waits for them, and re-layouts: 5.96 us -> 3.27 us
    pallas_call x0 -> x2, Pallas kernels: none -> 47.2 us  [the longest x1 27.6 us: body(): pl.pallas_call(functools.partial(gather_kernel, peers, groups_gx), out_sh...]
    reduce_scatter x1 -> x0, waiting for transfers between devices: 35.2 us -> none  [body(): lax.psum_scatter(jnp.einsum('mt,txc->mxc', own_columns, rhs, precision=la...]
    all_gather x1 -> x0, waiting for transfers between devices: 33.3 us -> none  [body(): lax.all_gather(solved, 'ta', axis=0, tiled=True)]
    add x27 -> x0, other arithmetic: 13.9 us -> none  [the longest x19 12.4 us: smooth(): field = field + DAMPING * (target - applied) / diag]
    dot_general x10 -> x0, matrix products: 11.6 us -> none  [the longest x4 3.77 us: restrict(): jnp.einsum('mgxc,cd->mgxd', paired, table, precision=lax.Precision.HIGHEST)]
    ppermute x2 -> x0, waiting for transfers between devices: 4.75 us -> none  [the longest x1 3.92 us: extended(): lax.ppermute(lax.slice_in_dim(block, 0, width, axis=dim), axis, backward)]
    ppermute x2 -> x0, starting transfers between devices: 3.69 us -> none  [the longest x1 2.4 us: extended(): lax.ppermute(lax.slice_in_dim(block, block.shape[dim] - width, None, axis...]
    sub x4 -> x0, other arithmetic: 2.91 us -> none  [vcycle(): resid = target - (diag * field - scale * neighbour_sum(field, zdim, ydim))]
  transfers between devices with their start and end apart: 4 -> 0, of which waited for: 4 -> 0; matrix products, arithmetic and copies ran while one was open for 0% -> 0% of each run, Pallas kernels for 0% -> 0%
where the time goes in v1:
time: 51.7 us; the launch traced here: 51.1 us
  Pallas kernels  47.2 us (91%)
  local copies, waits for them, and re-layouts  3.27 us (6%)
  other arithmetic  0.67 us (1%)
    pallas_call x1, Pallas kernels, body(): pl.pallas_call(functools.partial(gather_kernel, peers, groups_gx), out_sh...  27.6 us
    pallas_call x1, Pallas kernels, body(): pl.pallas_call(functools.partial(solve_kernel, peers, groups_gx), out_sha...  19.6 us
    unnamed x8, local copies, waits for them, and re-layouts  3.17 us

profile of v1, /device:TPU:0, one launch (start us, length us, event | category | flops | bytes accessed | tf_op | source)
XLA Modules:
  0.0 51.1 jit_solution(17438127380420910741)
XLA Ops:
  0.0 0.0 copy-start.3
  0.0 0.7 %exponential_multiply_fusion = f32[16]{0:T(128)S(1)} fusion(s32[16]{0:T(128)} %param.9), kind=kLoop, calls=%fused_computation | loop fusion | flops 48 | bytes 128 | tf_op jit(solution)/shard_map/mul | solution.py:487
  0.7 0.1 broadcast_in_dim.7
  0.8 0.0 copy-start
  0.8 1.2 %copy-done = f32[16,32,512]{2,1,0:T(8,128)S(1)} copy-done((f32[16,32,512]{2,1,0:T(8,128)S(1)}, f32[16,32,512]{2,1,0:T(8,128)}, u32[]{:S(2)}) %copy-start) | copy-done | bytes 1048600
  2.0 0.0 copy-start.1
  2.0 1.2 %copy-done.1 = f32[16,32,512]{2,1,0:T(8,128)S(1)} copy-done((f32[16,32,512]{2,1,0:T(8,128)S(1)}, f32[16,32,512]{2,1,0:T(8,128)}, u32[]{:S(2)}) %copy-start.1) | copy-done | bytes 1048600
  3.2 0.0 copy-start.2
  3.2 0.7 %copy-done.2 = f32[32,32]{1,0:T(8,128)S(1)} copy-done((f32[32,32]{1,0:T(8,128)S(1)}, f32[32,32]{1,0:T(8,128)}, u32[]{:S(2)}) %copy-start.2) | copy-done | bytes 4120
  3.9 27.6 %gather.1 = (f32[1,4,2,8,64,128]{5,4,3,2,1,0:T(8,128)S(1)}, f32[2,8,128]{2,1,0:T(8,128)S(1)}) custom-call(f32[16,32,512]{2,1,0:T(8,128)S(1)} %copy-done, f32[16,32,512]{2,1,0:T(8,128)S(1)} %copy-done.1, f32[8,128]{1,0:T(8,128)S(1)} %broadcast_in_dim.8.shift, f32[1,32,32]{2,1,0:T(8,128)S(1)} %bitcast.2), custom_call_target="tpu_custom_call" | custom-call | tf_op jit(solution)/shard_map/gather/pallas_call | solution.py:494
  31.5 0.0 copy-done.3
  31.5 19.6 %solve.1 = f32[16,32,512]{2,1,0:T(8,128)} custom-call(f32[1,4,2,8,64,128]{5,4,3,2,1,0:T(8,128)S(1)} %get-tuple-element.7.f_ref, f32[2,8,128]{2,1,0:T(8,128)S(1)} %get-tuple-element.8.shift, f32[1,32,32]{2,1,0:T(8,128)S(1)} %bitcast.3), custom_call_target="tpu_custom_call" | custom-call | tf_op jit(solution)/shard_map/solve/pallas_call | solution.py:523
  (2 shorter events, 0.0 us)
Async XLA Ops:
  0.0 31.5 %copy-start.3 = (f32[32,32]{1,0:T(8,128)S(1)}, f32[32,32]{1,0:T(8,128)}, u32[]{:S(2)}) copy-start(f32[32,32]{1,0:T(8,128)} %param.8) | copy-start | bytes 12292
  0.8 1.2 %copy-start = (f32[16,32,512]{2,1,0:T(8,128)S(1)}, f32[16,32,512]{2,1,0:T(8,128)}, u32[]{:S(2)}) copy-start(f32[16,32,512]{2,1,0:T(8,128)} %src.1) | copy-start | bytes 3145732
  2.0 1.2 %copy-start.1 = (f32[16,32,512]{2,1,0:T(8,128)S(1)}, f32[16,32,512]{2,1,0:T(8,128)}, u32[]{:S(2)}) copy-start(f32[16,32,512]{2,1,0:T(8,128)} %prev.1) | copy-start | bytes 3145732
  3.2 0.7 %copy-start.2 = (f32[32,32]{1,0:T(8,128)S(1)}, f32[32,32]{1,0:T(8,128)}, u32[]{:S(2)}) copy-start(f32[32,32]{1,0:T(8,128)} %param.7) | copy-start | bytes 12292

commit v2 on v1

--- a/solution.py
+++ b/solution.py
@@ -359,7 +359,7 @@
         def add0(ref):
             def body(zc, carry):
                 for g in range(chunks):
-                    value = center_all(u1a, g, zc, y1)
+                    value = center_all(u1b, g, zc, y1)
                     up0[g, zc, pl.ds(0, y1, stride=2), :] = value
                     up0[g, zc, pl.ds(1, y1, stride=2), :] = value
                 for g in range(chunks):
@@ -448,9 +448,6 @@
             add1(u1b)
             sweep(around1, u1b, u1a, g1, w1, 0.25, z1, y1)
             sweep(around1, u1a, u1b, g1, w1, 0.25, z1, y1)
-            for g in range(chunks):
-                for z in range(z1):
-                    u1a[g, z + 1, SUB : SUB + y1] = u1b[g, z + 1, SUB : SUB + y1]
             add0(vb)
             sweep0(vb, va)
             sweep0(va, vb)
@@ -487,7 +484,7 @@
     shifts = 0.05 * jnp.exp2(step_code.astype(jnp.float32) / 4.0)
     shifts = jnp.broadcast_to(jnp.tile(shifts, LANES // steps)[None], (SUB, LANES))
     vmem = pl.BlockSpec(memory_space=pltpu.VMEM)
-    anywhere = pl.BlockSpec(memory_space=pl.ANY)
+    anywhere = pl.BlockSpec(memory_space=pltpu.HBM)
     dma = pltpu.SemaphoreType.DMA
     f32 = jnp.float32
     field = (parts, chunks, 2, CZ, CY, LANES)
@@ -508,7 +505,7 @@
             pltpu.VMEM((parts, peers, steps * SUB, SUB * GROUP), f32),
         ] + [dma((peers,))] * 8 + [dma((2,)), dma((2,)), dma((3,))],
         compiler_params=pltpu.CompilerParams(
-            collective_id=0, has_side_effects=True, vmem_limit_bytes=48 << 20
+            collective_id=0, has_side_effects=True, vmem_limit_bytes=60 << 20
         ),
         name="gather",
     )(source, previous, shifts, time_modes.reshape(parts, GROUP, total))

time: 51.7 us -> 52.8 us (1.021)
  Pallas kernels: 47.2 us -> 48.5 us
    pallas_call x1, Pallas kernels: 27.6 us -> 29.7 us  [body(): pl.pallas_call(functools.partial(gather_kernel, peers, groups_gx), out_sh...]
    unnamed x8 -> x6, local copies, waits for them, and re-layouts: 3.17 us -> 2.28 us
    pallas_call x1, Pallas kernels: 19.6 us -> 18.8 us  [body(): pl.pallas_call(functools.partial(solve_kernel, peers, groups_gx), out_sha...]
    broadcast_in_dim x2, local copies, waits for them, and re-layouts: 0.09 us -> 0.69 us  [body(): jnp.broadcast_to(jnp.tile(shifts, LANES // steps)[None], (SUB, LANES))]
where the time goes in v2:
time: 52.8 us; the launch traced here: 52.2 us
  Pallas kernels  48.5 us (92%)
  local copies, waits for them, and re-layouts  2.97 us (6%)
  other arithmetic  0.67 us (1%)
    pallas_call x1, Pallas kernels, body(): pl.pallas_call(functools.partial(gather_kernel, peers, groups_gx), out_sh...  29.7 us
    pallas_call x1, Pallas kernels, body(): pl.pallas_call(functools.partial(solve_kernel, peers, groups_gx), out_sha...  18.8 us
    unnamed x6, local copies, waits for them, and re-layouts  2.28 us

profile of v2, /device:TPU:0, one launch (start us, length us, event | category | flops | bytes accessed | tf_op | source)
XLA Modules:
  0.0 52.2 jit_solution(2248161436357680111)
XLA Ops:
  0.0 0.0 copy-start.1
  0.0 0.7 %exponential_multiply_fusion = f32[16]{0:T(128)S(1)} fusion(s32[16]{0:T(128)} %param.9), kind=kLoop, calls=%fused_computation | loop fusion | flops 48 | bytes 128 | tf_op jit(solution)/shard_map/mul | solution.py:484
  0.7 0.1 broadcast_in_dim.7
  0.8 0.6 %broadcast_in_dim.8.shift = f32[8,128]{1,0:T(8,128)} broadcast(f32[128]{0:T(128)S(1)} %broadcast_in_dim.7), dimensions={1} | broadcast | bytes 4608 | tf_op jit(solution)/shard_map/broadcast_in_dim | solution.py:485
  1.4 29.7 %gather.1 = (f32[1,4,2,8,64,128]{5,4,3,2,1,0:T(8,128)}, f32[2,8,128]{2,1,0:T(8,128)}) custom-call(f32[16,32,512]{2,1,0:T(8,128)} %src.1, f32[16,32,512]{2,1,0:T(8,128)} %prev.1, f32[8,128]{1,0:T(8,128)} %broadcast_in_dim.8.shift, f32[1,32,32]{2,1,0:T(8,128)} %bitcast.3), custom_call_target="tpu_custom_call" | custom-call | tf_op jit(solution)/shard_map/gather/pallas_call | solution.py:491
  31.1 0.0 copy-done.1
  31.1 0.0 copy-start
  31.1 1.6 %copy-done = f32[1,4,2,8,64,128]{5,4,3,2,1,0:T(8,128)S(1)} copy-done((f32[1,4,2,8,64,128]{5,4,3,2,1,0:T(8,128)S(1)}, f32[1,4,2,8,64,128]{5,4,3,2,1,0:T(8,128)}, u32[]{:S(2)}) %copy-start) | copy-done | bytes 2097176
  32.7 0.0 copy-start.2
  32.7 0.7 %copy-done.2 = f32[2,8,128]{2,1,0:T(8,128)S(1)} copy-done((f32[2,8,128]{2,1,0:T(8,128)S(1)}, f32[2,8,128]{2,1,0:T(8,128)}, u32[]{:S(2)}) %copy-start.2) | copy-done | bytes 8216
  33.4 18.8 %solve.1 = f32[16,32,512]{2,1,0:T(8,128)} custom-call(f32[1,4,2,8,64,128]{5,4,3,2,1,0:T(8,128)S(1)} %copy-done, f32[2,8,128]{2,1,0:T(8,128)S(1)} %copy-done.2, f32[1,32,32]{2,1,0:T(8,128)S(1)} %bitcast.2), custom_call_target="tpu_custom_call" | custom-call | tf_op jit(solution)/shard_map/solve/pallas_call | solution.py:520
  (1 shorter events, 0.0 us)
Async XLA Ops:
  0.0 31.1 %copy-start.1 = (f32[32,32]{1,0:T(8,128)S(1)}, f32[32,32]{1,0:T(8,128)}, u32[]{:S(2)}) copy-start(f32[32,32]{1,0:T(8,128)} %param.8) | copy-start | bytes 12292
  31.1 1.6 %copy-start = (f32[1,4,2,8,64,128]{5,4,3,2,1,0:T(8,128)S(1)}, f32[1,4,2,8,64,128]{5,4,3,2,1,0:T(8,128)}, u32[]{:S(2)}) copy-start(f32[1,4,2,8,64,128]{5,4,3,2,1,0:T(8,128)} %get-tuple-element.7.f_ref) | copy-start | bytes 6291460
  32.7 0.7 %copy-start.2 = (f32[2,8,128]{2,1,0:T(8,128)S(1)}, f32[2,8,128]{2,1,0:T(8,128)}, u32[]{:S(2)}) copy-start(f32[2,8,128]{2,1,0:T(8,128)} %get-tuple-element.8.shift) | copy-start | bytes 24580
